TPU v7x, 512 devices: a whole 4x8x8 slice. The times are simulated.
512 devices in a mesh: ent: 128 (over y, z, core), rep: 4 (over x).
Axes of the slice: x: 4, y: 8, z: 8, core: 2. Of those that a mesh axis runs over, the one named last changes fastest.
Arguments:
- entity_table: float32 [65536, 200], P('ent'), may hold values from -6 to 6
- relation_table: bfloat16 [822, 200], replicated, may hold values from -12 to 12
- filters: float32 [32, 9], replicated, may hold values from -2 to 2
- projection: bfloat16 [9728, 200], replicated, may hold values from -0.0625 to 0.0625
- request_owner: int32 [163840, 1], P(('ent', 'rep')), may hold values from 0 to 127; in each aligned block of 320 rows (0 to 319, 320 to 639, ...) at most 4 rows name the same one
- request_row: int32 [163840], P(('ent', 'rep')), may hold values from 0 to 511
- relation_id: int32 [65536], P(('ent', 'rep')), may hold values from 0 to 821
- rare_flag: int32 [65536], P('ent'), may hold values 0 or 1
- running_norm: float32 [], replicated, may hold values from 2 to 6
Outputs:
- new_table: float32 [65536, 200], P('ent')
- filter_grad: float32 [32, 9], replicated
Inputs may be any that keep to these rules, and one draw needn't show every extreme that they name: `request_owner`: among the requests of one device no owner shard is named more than 4 times, a bound that some block reaches.
All inputs are finite; a program needn't handle non-finite values. No bound on the sum of `rare_flag` on one device may be relied on, other than what follows from the above.
Results may differ from a plain program's by a relative error of at most 0.002.
Values sent between devices are 32-bit elements; how exact they have to be, the bound alone decides.
A program may use at most 64 MiB of HBM per device.

v0:
```python
import jax
import jax.numpy as jnp
from jax import lax
from jax.sharding import PartitionSpec as P

D = 200
ROWS = 20
learn_rate = 0.5
norm_eps = 1e-06


def conv_act(head_rows, rel_rows, filters):
    count = head_rows.shape[0]
    stacked = jnp.concatenate(
        [head_rows.reshape(count, ROWS, D // ROWS), rel_rows.reshape(count, ROWS, D // ROWS)],
        axis=1,
    )[:, None]
    kernel = filters.reshape(filters.shape[0], 1, 3, 3)
    conv_out = lax.conv_general_dilated(
        stacked, kernel, (1, 1), "VALID", precision=lax.Precision.HIGHEST
    )
    return jax.nn.silu(conv_out).reshape(count, -1)


def block_step(row_values, rel_rows, filters, projection, batch_rows, neg_count):
    head_rows = row_values[:batch_rows]
    pos_rows = row_values[batch_rows : 2 * batch_rows]
    neg_rows = row_values[2 * batch_rows :]
    activated, pullback = jax.vjp(
        lambda head_part, filt_part: conv_act(head_part, rel_rows, filt_part), head_rows, filters
    )
    features = activated.astype(jnp.bfloat16)
    projected = jnp.dot(features, projection, preferred_element_type=jnp.float32)
    sig_proj = jax.nn.sigmoid(projected)
    hidden = projected * sig_proj
    score_pos = jnp.sum(hidden * pos_rows, 1)
    score_neg = jnp.dot(hidden, neg_rows.T, precision=lax.Precision.HIGHEST)
    grad_pos = -jax.nn.sigmoid(-score_pos)
    grad_neg = jax.nn.sigmoid(score_neg) / neg_count
    pos_grad_rows = grad_pos[:, None] * hidden
    neg_grad_rows = jnp.dot(grad_neg.T, hidden, precision=lax.Precision.HIGHEST)
    grad_hidden = grad_pos[:, None] * pos_rows + jnp.dot(
        grad_neg, neg_rows, precision=lax.Precision.HIGHEST
    )
    grad_proj = (grad_hidden * sig_proj * (1.0 + projected * (1.0 - sig_proj))).astype(jnp.bfloat16)
    grad_feat = lax.dot_general(
        grad_proj, projection, (((1,), (1,)), ((), ())), preferred_element_type=jnp.float32
    )
    head_grad_rows, filter_part = pullback(grad_feat)
    return (jnp.concatenate([head_grad_rows, pos_grad_rows, neg_grad_rows], axis=0), filter_part)


def body(
    entity_table,
    relation_table,
    filters,
    projection,
    request_owner,
    request_row,
    relation_id,
    rare_flag,
    running_norm,
):
    ent_count = lax.axis_size("ent")
    rep_count = lax.axis_size("rep")
    req_count = request_row.shape[0]
    batch_rows = relation_id.shape[0]
    neg_count = req_count - 2 * batch_rows
    width = entity_table.shape[1]
    slots_each = max(2, 3 * req_count // (2 * ent_count) + 1)
    owner_shard = request_owner[:, 0]
    onehot = (owner_shard[:, None] == jnp.arange(ent_count, dtype=jnp.int32)[None, :]).astype(
        jnp.int32
    )
    slot_index = jnp.sum(jnp.cumsum(onehot, 0) * onehot, 1) - 1
    slot_place = owner_shard * slots_each + slot_index
    send_ids = (
        jnp.zeros((ent_count * slots_each,), jnp.int32)
        .at[slot_place]
        .set(request_row)
        .reshape(ent_count, slots_each)
    )
    wanted = lax.all_to_all(send_ids, "ent", split_axis=0, concat_axis=0, tiled=True)
    found_rows = entity_table[wanted]
    fetched = lax.all_to_all(found_rows, "ent", split_axis=0, concat_axis=0, tiled=True)
    row_values = fetched.reshape(-1, width)[slot_place]
    rel_rows = relation_table[relation_id].astype(jnp.float32)
    grads, filter_part = block_step(
        row_values, rel_rows, filters, projection, batch_rows, neg_count
    )
    send_grads = (
        jnp.zeros((ent_count * slots_each, width), jnp.float32)
        .at[slot_place]
        .set(grads)
        .reshape(ent_count, slots_each, width)
    )
    received = lax.all_to_all(send_grads, "ent", split_axis=0, concat_axis=0, tiled=True)
    all_ids = lax.all_gather(wanted, "rep", axis=0, tiled=True)
    all_grads = lax.all_gather(received, "rep", axis=0, tiled=True)
    summed_grad = (
        jnp.zeros(entity_table.shape, jnp.float32)
        .at[all_ids.reshape(-1)]
        .add(all_grads.reshape(-1, width))
    )
    updated = entity_table - learn_rate * summed_grad
    row_norms = jnp.sqrt(jnp.sum(updated * updated, 1) + norm_eps)
    local_norm = jnp.sum(row_norms)
    filter_total = lax.psum(filter_part, ("ent", "rep"))
    norm_total = lax.psum(local_norm, "ent")
    filter_grad = filter_total / (batch_rows * ent_count * rep_count)
    target = 0.25 * running_norm + 0.75 * norm_total / (entity_table.shape[0] * ent_count)
    new_table = jnp.where(
        (rare_flag == 1)[:, None], updated * (target / row_norms)[:, None], updated
    )
    return (new_table, filter_grad)


def solution(mesh):
    in_specs = (
        P("ent", None),
        P(),
        P(),
        P(),
        P(("ent", "rep"), None),
        P(("ent", "rep")),
        P(("ent", "rep")),
        P("ent"),
        P(),
    )
    out_specs = (P("ent", None), P())
    return jax.shard_map(body, mesh=mesh, in_specs=in_specs, out_specs=out_specs, check_vma=False)
```

profile of v0, /device:TPU:1, one launch (start us, length us, event | category | flops | bytes accessed | tf_op | source)
XLA Modules:
  0.0 538.2 jit_solution(8350565503353187962)
XLA Ops:
  9.2 3.1 scatter_custom_fusion
  13.1 18.4 %all-to-all-start = ((s32[128,1,4]{2,1,0:T(1,128)}), s32[128,1,4]{2,1,0:T(1,128)S(1)}, u32[]{:S(2)}, u32[]{:S(2)}) async-start(s32[128,1,4]{2,1,0:T(1,128)} %bitcast.4), calls=%async_computation | async-start | bytes 131072 | tf_op jit(solution)/shard_map/all_to_all | solution.py:83
  31.5 1.2 copy.117
  32.7 10.2 %all-to-all-done = s32[128,1,4]{2,1,0:T(1,128)S(1)} async-done(((s32[128,1,4]{2,1,0:T(1,128)}), s32[128,1,4]{2,1,0:T(1,128)S(1)}, u32[]{:S(2)}, u32[]{:S(2)}) %all-to-all-start) | async-done | bytes 2080 | tf_op jit(solution)/shard_map/all_to_all | solution.py:83
  43.6 1.6 gather_fusion
  46.1 5.7 %all-to-all-start.1 = ((f32[128,4,200]{2,1,0:T(4,128)}), f32[128,4,200]{2,1,0:T(4,128)S(1)}, u32[]{:S(2)}, u32[]{:S(2)}) async-start(f32[128,4,200]{2,1,0:T(4,128)} %reshape.144), calls=%async_computation.1 | async-start | bytes 1048576 | tf_op jit(solution)/shard_map/all_to_all | solution.py:85
  53.6 17.8 %all-to-all-done.1 = f32[128,4,200]{2,1,0:T(4,128)S(1)} async-done(((f32[128,4,200]{2,1,0:T(4,128)}), f32[128,4,200]{2,1,0:T(4,128)S(1)}, u32[]{:S(2)}, u32[]{:S(2)}) %all-to-all-start.1) | async-done | bytes 409632 | tf_op jit(solution)/shard_map/all_to_all | solution.py:85
  71.6 1.6 gather_fusion.1
  74.1 7.1 %multiply_convert_fusion = (bf16[128,32,38,8]{0,1,3,2:T(8,128)(2,1)S(1)}, f32[128,32,38,8]{0,1,3,2:T(8,128)}) fusion(f32[32,1,3,3]{0,1,3,2:T(1,128)S(1)} %reshape.195, f32[128,1,40,10]{0,2,3,1:T(8,128)S(1)} %bitcast.46), kind=kOutput, calls=%fused_computation.9 | convolution fusion | flops 140705792 | bytes 7677056 | tf_op jit(solution)/shard_map/jvp()/conv_general_dilated | solution.py:19
  82.1 1.6 copy.123
  83.8 3.5 multiply_reduce_fusion.1
  88.3 2.0 fusion.30
  90.4 2.6 fusion.1
  93.1 2.2 copy-done
  95.3 23.1 %fusion.29 = f32[128,1,40,10]{0,1,3,2:T(1,128)S(1)} fusion(f32[128,32,38,8]{0,1,3,2:T(8,128)S(1)} %fusion.1, f32[32,1,3,3]{0,1,3,2:T(1,128)S(1)} %reshape.195), kind=kOutput, calls=%fused_computation.68 | convolution fusion | flops 134479872 | bytes 5186688 | tf_op jit(solution)/shard_map/transpose(jvp())/conv_general_dilated | solution.py:19
  118.7 1.9 scatter_custom_fusion.1
  120.7 26.3 %all_to_all.25 = f32[128,4,200]{2,1,0:T(4,128)S(1)} all-to-all(f32[128,4,200]{2,1,0:T(4,128)S(1)} %reshape.138), channel_id=1, replica_groups=mesh['ent'=128,'rep'=4] {'ent'}, dimensions={0} | all-to-all | bytes 819200 | tf_op jit(solution)/shard_map/all_to_all | solution.py:97
  148.7 8.4 %all-gather = s32[512,1,4]{0,2,1:T(4,128)S(1)} all-gather(s32[128,1,4]{0,2,1:T(4,128)S(1)} %copy.96), channel_id=2, replica_groups=mesh['ent'=128,'rep'=4] {'rep'}, dimensions={0}, use_global_device_ids=true | all-gather | bytes 10240 | tf_op jit(solution)/shard_map/all_gather | solution.py:98
  157.5 9.4 %convolution_reduce_fusion = f32[32,3,3]{0,2,1:T(4,128)S(1)} fusion(f32[128,32,38,8]{0,1,3,2:T(8,128)} %copy-done, f32[128,1,40,10]{0,2,3,1:T(8,128)S(1)} %bitcast.47), kind=kOutput, calls=%fused_computation.20 | convolution fusion | flops 134479872 | bytes 5186688 | tf_op jit(solution)/shard_map/transpose(jvp())/conv_general_dilated | solution.py:19
  166.9 97.7 %psum.15 = f32[32,9]{0,1:T(8,128)S(1)} all-reduce(f32[32,9]{0,1:T(8,128)S(1)} %reshape.140), channel_id=1, replica_groups=mesh['ent'=128,'rep'=4] {'ent','rep'}, use_global_device_ids=true, to_apply=%region_10.11 | all-reduce | flops 288 | bytes 2304 | tf_op jit(solution)/shard_map/psum | solution.py:108
  264.6 2.0 copy.116
  266.6 1.8 reshape.187
  268.3 12.1 %scatter_custom_fusion.2 = f32[512,200]{1,0:T(8,128)S(1)} fusion(s32[2048]{0:T(1024)S(1)} %bitcast.53, f32[2048,200]{1,0:T(8,128)} %reshape.187, f32[]{:T(128)} %constant.16.clone.1), kind=kCustom, calls=%fused_computation.28 | custom fusion | flops 409600 | bytes 410112 | tf_op jit(solution)/shard_map/scatter-add | solution.py:103
  281.8 247.5 %psum.14 = f32[]{:T(128)} all-reduce(f32[]{:T(128)} %sqrt_reduce_fusion), channel_id=1, replica_groups=mesh['ent'=128,'rep'=4] {'ent'}, use_global_device_ids=true, to_apply=%region_9.10 | all-reduce | flops 1 | bytes 8 | tf_op jit(solution)/shard_map/psum | solution.py:109
  (83 shorter events, 13.4 us)
Async XLA Ops:
  8.0 44.3 %copy-start.5 = (bf16[822,200]{0,1:T(8,128)(2,1)S(1)}, bf16[822,200]{0,1:T(8,128)(2,1)}, u32[]{:S(2)}) copy-start(bf16[822,200]{0,1:T(8,128)(2,1)} %param.10) | copy-start | bytes 986404
  8.2 44.3 %copy-start.9 = (s32[128]{0:T(128)S(1)}, s32[128]{0:T(128)}, u32[]{:S(2)}) copy-start(s32[128]{0:T(128)} %param.15) | copy-start | bytes 1540
  8.5 45.1 %copy-start.6 = (f32[32,9]{0,1:T(8,128)S(1)}, f32[32,9]{0,1:T(8,128)}, u32[]{:S(2)}) copy-start(f32[32,9]{0,1:T(8,128)} %param.11) | copy-start | bytes 3460
  9.2 62.3 %copy-start.7 = (s32[320]{0:T(512)}, s32[320]{0:T(512)S(1)}, u32[]{:S(2)}) copy-start(s32[320]{0:T(512)S(1)} %fusion.22) | copy-start | bytes 3844
  13.1 29.9 %all-to-all-start = ((s32[128,1,4]{2,1,0:T(1,128)}), s32[128,1,4]{2,1,0:T(1,128)S(1)}, u32[]{:S(2)}, u32[]{:S(2)}) async-start(s32[128,1,4]{2,1,0:T(1,128)} %bitcast.4), calls=%async_computation | async-start | bytes 131072 | tf_op jit(solution)/shard_map/all_to_all | solution.py:83
  42.9 0.6 copy-start.2
  46.1 25.3 %all-to-all-start.1 = ((f32[128,4,200]{2,1,0:T(4,128)}), f32[128,4,200]{2,1,0:T(4,128)S(1)}, u32[]{:S(2)}, u32[]{:S(2)}) async-start(f32[128,4,200]{2,1,0:T(4,128)} %reshape.144), calls=%async_computation.1 | async-start | bytes 1048576 | tf_op jit(solution)/shard_map/all_to_all | solution.py:85
  51.8 212.8 %all-gather.3.cloned.1.call-start = ((), (), s32[]{:S(2)}) async-start(), calls=%async_computation.3 | async-start | bytes 2048000 | tf_op jit(solution)/shard_map/all_gather | solution.py:99
  83.8 4.1 copy-start.4
  83.8 4.5 copy-start.1
  87.5 2.8 slice-start
  88.3 2.1 slice-start.1
  93.1 2.2 copy-start
  95.3 53.4 %copy-start.8 = (s32[512]{0:T(512)S(1)}, s32[512]{0:T(512)}, u32[]{:S(2)}) copy-start(s32[512]{0:T(512)} %param.16) | copy-start | bytes 6148
  95.3 53.4 %copy-start.3 = (s32[128,1,4]{2,1,0:T(1,128)S(1)}, s32[128,1,4]{2,1,0:T(1,128)}, u32[]{:S(2)}) copy-start(s32[128,1,4]{2,1,0:T(1,128)} %copy-done.2) | copy-start | bytes 6148
Sparse Core Ops, SparseCore 0:
  148.1 28.8 all-gather.2
where the time goes:
time: 544 us; the launch traced here: 538 us
  blocking collectives  380 us (70%)
  matrix products  46 us (8%)
  waiting for transfers between devices  28 us (5%)
  local copies, waits for them, and re-layouts  25.1 us (5%)
  starting transfers between devices  24.6 us (5%)
  other arithmetic  18.4 us (3%)
  between operations  16.1 us (3%)
    psum x1, blocking collectives, body(): norm_total = lax.psum(local_norm, 'ent')  247 us
    psum x1, blocking collectives, body(): filter_total = lax.psum(filter_part, ('ent', 'rep'))  97.7 us
    conv_general_dilated x3, matrix products, conv_act(): lax.conv_general_dilated(stacked, kernel, (1, 1), 'VALID', precision=lax....  39.5 us
    all_to_all x1, blocking collectives, body(): lax.all_to_all(send_grads, 'ent', split_axis=0, concat_axis=0, tiled=True)  26.3 us
    all_to_all x1, starting transfers between devices, body(): lax.all_to_all(send_ids, 'ent', split_axis=0, concat_axis=0, tiled=True)  18.4 us
    all_to_all x1, waiting for transfers between devices, body(): lax.all_to_all(found_rows, 'ent', split_axis=0, concat_axis=0, tiled=True)  17.8 us
    scatter-add x1, other arithmetic, body(): summed_grad = jnp.zeros(entity_table.shape, jnp.float32).at[all_ids.resha...  12.1 us
  transfers between devices with their start and end apart: 3, of which 2 were waited for; matrix products, arithmetic and copies ran while one was open for 2% of the time, Pallas kernels for 0%

commit v1 on v0

--- a/solution.py
+++ b/solution.py
@@ -105,7 +105,7 @@
     updated = entity_table - learn_rate * summed_grad
     row_norms = jnp.sqrt(jnp.sum(updated * updated, 1) + norm_eps)
     local_norm = jnp.sum(row_norms)
-    filter_total = lax.psum(filter_part, ("ent", "rep"))
+    filter_total = lax.psum(lax.psum(filter_part, "rep"), "ent")
     norm_total = lax.psum(local_norm, "ent")
     filter_grad = filter_total / (batch_rows * ent_count * rep_count)
     target = 0.25 * running_norm + 0.75 * norm_total / (entity_table.shape[0] * ent_count)

time: 544 us -> 469 us (0.86)
  blocking collectives: 380 us -> 302 us
    psum x1, blocking collectives: 97.7 us -> 8.32 us  [body(): filter_total = lax.psum(lax.psum(filter_part, 'rep'), 'ent')]
    psum x1, blocking collectives: 247 us -> 259 us  [body(): norm_total = lax.psum(local_norm, 'ent')]
  transfers between devices with their start and end apart: 3 -> 3, of which waited for: 2 -> 3; matrix products, arithmetic and copies ran while one was open for 2% -> 3% of each run, Pallas kernels for 0% -> 0%
where the time goes in v1:
time: 469 us; the launch traced here: 462 us
  blocking collectives  302 us (64%)
  matrix products  46 us (10%)
  waiting for transfers between devices  29.8 us (6%)
  local copies, waits for them, and re-layouts  25.1 us (5%)
  starting transfers between devices  24.6 us (5%)
  other arithmetic  18.4 us (4%)
  between operations  16.1 us (3%)
    psum x1, blocking collectives, body(): norm_total = lax.psum(local_norm, 'ent')  259 us
    conv_general_dilated x3, matrix products, conv_act(): lax.conv_general_dilated(stacked, kernel, (1, 1), 'VALID', precision=lax....  39.5 us
    all_to_all x1, blocking collectives, body(): lax.all_to_all(send_grads, 'ent', split_axis=0, concat_axis=0, tiled=True)  26.3 us
    all_to_all x1, starting transfers between devices, body(): lax.all_to_all(send_ids, 'ent', split_axis=0, concat_axis=0, tiled=True)  18.4 us
    all_to_all x1, waiting for transfers between devices, body(): lax.all_to_all(found_rows, 'ent', split_axis=0, concat_axis=0, tiled=True)  17.8 us
    scatter-add x1, other arithmetic, body(): summed_grad = jnp.zeros(entity_table.shape, jnp.float32).at[all_ids.resha...  12.1 us
    all_to_all x1, waiting for transfers between devices, body(): lax.all_to_all(send_ids, 'ent', split_axis=0, concat_axis=0, tiled=True)  10.2 us
  transfers between devices with their start and end apart: 3, of which 3 were waited for; matrix products, arithmetic and copies ran while one was open for 3% of the time, Pallas kernels for 0%

profile of v1, /device:TPU:1, one launch (start us, length us, event | category | flops | bytes accessed | tf_op | source)
XLA Modules:
  0.0 461.9 jit_solution(11373424271101292609)
XLA Ops:
  9.2 3.1 scatter_custom_fusion
  13.1 18.4 %all-to-all-start = ((s32[128,1,4]{2,1,0:T(1,128)}), s32[128,1,4]{2,1,0:T(1,128)S(1)}, u32[]{:S(2)}, u32[]{:S(2)}) async-start(s32[128,1,4]{2,1,0:T(1,128)} %bitcast.4), calls=%async_computation | async-start | bytes 131072 | tf_op jit(solution)/shard_map/all_to_all | solution.py:83
  32.7 10.2 %all-to-all-done = s32[128,1,4]{2,1,0:T(1,128)S(1)} async-done(((s32[128,1,4]{2,1,0:T(1,128)}), s32[128,1,4]{2,1,0:T(1,128)S(1)}, u32[]{:S(2)}, u32[]{:S(2)}) %all-to-all-start) | async-done | bytes 2080 | tf_op jit(solution)/shard_map/all_to_all | solution.py:83
  43.6 1.6 gather_fusion
  46.1 5.7 %all-to-all-start.1 = ((f32[128,4,200]{2,1,0:T(4,128)}), f32[128,4,200]{2,1,0:T(4,128)S(1)}, u32[]{:S(2)}, u32[]{:S(2)}) async-start(f32[128,4,200]{2,1,0:T(4,128)} %reshape.144), calls=%async_computation.1 | async-start | bytes 1048576 | tf_op jit(solution)/shard_map/all_to_all | solution.py:85
  53.6 17.8 %all-to-all-done.1 = f32[128,4,200]{2,1,0:T(4,128)S(1)} async-done(((f32[128,4,200]{2,1,0:T(4,128)}), f32[128,4,200]{2,1,0:T(4,128)S(1)}, u32[]{:S(2)}, u32[]{:S(2)}) %all-to-all-start.1) | async-done | bytes 409632 | tf_op jit(solution)/shard_map/all_to_all | solution.py:85
  71.6 1.6 gather_fusion.1
  74.1 7.1 %multiply_convert_fusion = (bf16[128,32,38,8]{0,1,3,2:T(8,128)(2,1)S(1)}, f32[128,32,38,8]{0,1,3,2:T(8,128)}) fusion(f32[32,1,3,3]{0,1,3,2:T(1,128)S(1)} %reshape.195, f32[128,1,40,10]{0,2,3,1:T(8,128)S(1)} %bitcast.46), kind=kOutput, calls=%fused_computation.9 | convolution fusion | flops 140705792 | bytes 7677056 | tf_op jit(solution)/shard_map/jvp()/conv_general_dilated | solution.py:19
  82.1 1.6 copy.123
  83.8 3.5 multiply_reduce_fusion.1
  88.3 2.0 fusion.30
  90.4 2.6 fusion.1
  93.1 2.2 copy-done
  95.3 23.1 %fusion.29 = f32[128,1,40,10]{0,1,3,2:T(1,128)S(1)} fusion(f32[128,32,38,8]{0,1,3,2:T(8,128)S(1)} %fusion.1, f32[32,1,3,3]{0,1,3,2:T(1,128)S(1)} %reshape.195), kind=kOutput, calls=%fused_computation.68 | convolution fusion | flops 134479872 | bytes 5186688 | tf_op jit(solution)/shard_map/transpose(jvp())/conv_general_dilated | solution.py:19
  118.7 1.9 scatter_custom_fusion.1
  120.7 26.3 %all_to_all.25 = f32[128,4,200]{2,1,0:T(4,128)S(1)} all-to-all(f32[128,4,200]{2,1,0:T(4,128)S(1)} %reshape.138), channel_id=1, replica_groups=mesh['ent'=128,'rep'=4] {'ent'}, dimensions={0} | all-to-all | bytes 819200 | tf_op jit(solution)/shard_map/all_to_all | solution.py:97
  148.7 8.4 %all-gather = s32[512,1,4]{0,2,1:T(4,128)S(1)} all-gather(s32[128,1,4]{0,2,1:T(4,128)S(1)} %copy.96), channel_id=2, replica_groups=mesh['ent'=128,'rep'=4] {'rep'}, dimensions={0}, use_global_device_ids=true | all-gather | bytes 10240 | tf_op jit(solution)/shard_map/all_gather | solution.py:98
  157.5 9.4 %convolution_reduce_fusion = f32[32,3,3]{0,2,1:T(4,128)S(1)} fusion(f32[128,32,38,8]{0,1,3,2:T(8,128)} %copy-done, f32[128,1,40,10]{0,2,3,1:T(8,128)S(1)} %bitcast.47), kind=kOutput, calls=%fused_computation.20 | convolution fusion | flops 134479872 | bytes 5186688 | tf_op jit(solution)/shard_map/transpose(jvp())/conv_general_dilated | solution.py:19
  166.9 8.3 %psum.22 = f32[32,9]{0,1:T(8,128)S(1)} all-reduce(f32[32,9]{0,1:T(8,128)S(1)} %reshape.140), channel_id=1, replica_groups=mesh['ent'=128,'rep'=4] {'rep'}, use_global_device_ids=true, to_apply=%region_10.11 | all-reduce | flops 288 | bytes 2304 | tf_op jit(solution)/shard_map/psum | solution.py:108
  175.2 1.8 all-gather.3.cloned.1.call-done
  177.0 2.0 copy.116
  179.0 1.8 reshape.187
  180.7 12.1 %scatter_custom_fusion.2 = f32[512,200]{1,0:T(8,128)S(1)} fusion(s32[2048]{0:T(1024)S(1)} %bitcast.53, f32[2048,200]{1,0:T(8,128)} %reshape.187, f32[]{:T(128)} %constant.16.clone.1), kind=kCustom, calls=%fused_computation.28 | custom fusion | flops 409600 | bytes 410112 | tf_op jit(solution)/shard_map/scatter-add | solution.py:103
  193.6 258.8 %all-reduce.1 = (f32[]{:T(128)}, f32[32,9]{0,1:T(8,128)S(1)}) all-reduce(f32[]{:T(128)} %sqrt_reduce_fusion, f32[32,9]{0,1:T(8,128)S(1)} %psum.22), channel_id=1, replica_groups=mesh['ent'=128,'rep'=4] {'ent'}, use_global_device_ids=true, to_apply=%region_9.10 | all-reduce | flops 289 | bytes 2312 | tf_op jit(solution)/shard_map/psum | solution.py:109
  (83 shorter events, 14.6 us)
Async XLA Ops:
  8.0 44.3 %copy-start.5 = (bf16[822,200]{0,1:T(8,128)(2,1)S(1)}, bf16[822,200]{0,1:T(8,128)(2,1)}, u32[]{:S(2)}) copy-start(bf16[822,200]{0,1:T(8,128)(2,1)} %param.10) | copy-start | bytes 986404
  8.2 44.3 %copy-start.9 = (s32[128]{0:T(128)S(1)}, s32[128]{0:T(128)}, u32[]{:S(2)}) copy-start(s32[128]{0:T(128)} %param.15) | copy-start | bytes 1540
  8.5 45.1 %copy-start.6 = (f32[32,9]{0,1:T(8,128)S(1)}, f32[32,9]{0,1:T(8,128)}, u32[]{:S(2)}) copy-start(f32[32,9]{0,1:T(8,128)} %param.11) | copy-start | bytes 3460
  9.2 62.3 %copy-start.7 = (s32[320]{0:T(512)}, s32[320]{0:T(512)S(1)}, u32[]{:S(2)}) copy-start(s32[320]{0:T(512)S(1)} %fusion.22) | copy-start | bytes 3844
  13.1 29.9 %all-to-all-start = ((s32[128,1,4]{2,1,0:T(1,128)}), s32[128,1,4]{2,1,0:T(1,128)S(1)}, u32[]{:S(2)}, u32[]{:S(2)}) async-start(s32[128,1,4]{2,1,0:T(1,128)} %bitcast.4), calls=%async_computation | async-start | bytes 131072 | tf_op jit(solution)/shard_map/all_to_all | solution.py:83
  42.9 0.6 copy-start.2
  46.1 25.3 %all-to-all-start.1 = ((f32[128,4,200]{2,1,0:T(4,128)}), f32[128,4,200]{2,1,0:T(4,128)S(1)}, u32[]{:S(2)}, u32[]{:S(2)}) async-start(f32[128,4,200]{2,1,0:T(4,128)} %reshape.144), calls=%async_computation.1 | async-start | bytes 1048576 | tf_op jit(solution)/shard_map/all_to_all | solution.py:85
  51.8 125.2 %all-gather.3.cloned.1.call-start = ((), (), s32[]{:S(2)}) async-start(), calls=%async_computation.3 | async-start | bytes 2048000 | tf_op jit(solution)/shard_map/all_gather | solution.py:99
  83.8 4.1 copy-start.4
  83.8 4.5 copy-start.1
  87.5 2.8 slice-start
  88.3 2.1 slice-start.1
  93.1 2.2 copy-start
  95.3 53.4 %copy-start.8 = (s32[512]{0:T(512)S(1)}, s32[512]{0:T(512)}, u32[]{:S(2)}) copy-start(s32[512]{0:T(512)} %param.16) | copy-start | bytes 6148
  95.3 53.4 %copy-start.3 = (s32[128,1,4]{2,1,0:T(1,128)S(1)}, s32[128,1,4]{2,1,0:T(1,128)}, u32[]{:S(2)}) copy-start(s32[128,1,4]{2,1,0:T(1,128)} %copy-done.2) | copy-start | bytes 6148
Sparse Core Ops, SparseCore 0:
  148.1 28.8 all-gather.2
